TPU v7x, 512 devices: a whole 4x8x8 slice. The times are simulated.
512 devices in a mesh: dp: 64 (over z, y_hi, x), shard: 8 (over y_lo, core).
Axes of the slice: x: 4, y: 8 (y_hi: 2, y_lo: 4; y = y_hi * 4 + y_lo), z: 8, core: 2. Of those that a mesh axis runs over, the one named last changes fastest.
Arguments:
- inputs: bfloat16 [512, 8, 8, 8, 256], P(('dp', 'shard')), may hold values from -24 to 24
- cotangent: bfloat16 [512, 4, 4, 4, 256], P(('dp', 'shard')), may hold values from -6 to 6
- weights: bfloat16 [28, 256, 256], P(None, 'shard'), may hold values from -0.078125 to 0.078125
Outputs:
- outputs: bfloat16 [512, 4, 4, 4, 256], P(('dp', 'shard'))
- input_grad: bfloat16 [512, 8, 8, 8, 256], P(('dp', 'shard'))
- weight_grad: float32 [28, 256, 256], P(None, 'shard')
All inputs are finite; a program needn't handle non-finite values.
Results may differ from a plain program's by a relative error of at most 0.012.
Values may be sent and summed in bfloat16 or wider, within the bound.
A program may use at most 64 MiB of HBM per device.

v0:
```python
import jax
import jax.numpy as jnp
from jax import lax
from jax.sharding import PartitionSpec as P


def build_cols(values):
    edge = values.shape[0]
    half = edge // 2
    width = values.shape[3]
    act = jax.nn.silu(values.astype(jnp.float32)).astype(jnp.bfloat16)
    padded = jnp.pad(act, ((1, 1), (1, 1), (1, 1), (0, 0)))
    pieces = []
    for first in range(3):
        for second in range(3):
            for third in range(3):
                pieces.append(
                    padded[
                        first : first + edge : 2,
                        second : second + edge : 2,
                        third : third + edge : 2,
                    ]
                )
    pieces.append(values[0::2, 0::2, 0::2])
    return jnp.stack(pieces, axis=3).reshape(half * half * half, 28, width)


def spread_back(values, grad_rows, piece, half):
    width = piece.shape[1]
    edge = 2 * half
    grid = jnp.zeros((edge + 2, edge + 2, edge + 2, width), jnp.float32)
    for first in range(3):
        block = jnp.einsum(
            "qo,tco->qtc",
            grad_rows,
            piece[9 * first : 9 * first + 9],
            preferred_element_type=jnp.float32,
        )
        block = block.reshape(half, half, half, 9, width)
        for second in range(3):
            for third in range(3):
                grid = grid.at[
                    first : first + edge : 2, second : second + edge : 2, third : third + edge : 2
                ].add(block[:, :, :, 3 * second + third])
    direct = jnp.einsum(
        "qo,co->qc", grad_rows, piece[27], preferred_element_type=jnp.float32
    ).reshape(half, half, half, width)
    own = values.astype(jnp.float32)
    sigma = jax.nn.sigmoid(own)
    grad_in = grid[1:-1, 1:-1, 1:-1] * sigma * (1.0 + own * (1.0 - sigma))
    grad_in = grad_in.at[0::2, 0::2, 0::2].add(direct)
    return grad_in.astype(jnp.bfloat16)


def shards(inputs, cotangent, weights):
    values = inputs[0]
    edge = values.shape[0]
    half = edge // 2
    chans = values.shape[3]
    taps_count = weights.shape[0]
    cols = build_cols(values)
    grad_rows = cotangent[0].reshape(half * half * half, chans)
    result = jnp.einsum(
        "qtc,tco->qo",
        cols,
        lax.all_gather(weights, "shard", axis=1, tiled=True),
        preferred_element_type=jnp.float32,
    )
    grad_in = spread_back(
        values, grad_rows, lax.all_gather(weights, "shard", axis=1, tiled=True), half
    )
    term = lax.dot_general(
        cols.reshape(half * half * half, taps_count * chans),
        grad_rows,
        (((0,), (0,)), ((), ())),
        preferred_element_type=jnp.float32,
    )
    term = term.astype(jnp.bfloat16).astype(jnp.float32).reshape(taps_count, chans, chans)
    owned = lax.psum_scatter(
        term.astype(jnp.bfloat16), "shard", scatter_dimension=1, tiled=True
    ).astype(jnp.float32)
    weight_grad = lax.psum(owned, "dp")
    outputs = result.astype(jnp.bfloat16).reshape(1, half, half, half, chans)
    return (outputs, grad_in.reshape(1, edge, edge, edge, chans), weight_grad)


def solution(mesh):
    return jax.shard_map(
        shards,
        mesh=mesh,
        in_specs=(
            P(("dp", "shard"), None, None, None, None),
            P(("dp", "shard"), None, None, None, None),
            P(None, "shard", None),
        ),
        out_specs=(
            P(("dp", "shard"), None, None, None, None),
            P(("dp", "shard"), None, None, None, None),
            P(None, "shard", None),
        ),
        check_vma=False,
    )
```

profile of v0, /device:TPU:8, one launch (start us, length us, event | category | flops | bytes accessed | tf_op | source)
XLA Modules:
  0.0 727.1 jit_solution(8520491467379494696)
XLA Ops:
  10.8 5.8 slice.207
  17.4 45.1 %all-gather.2.cloned.1.call-done = bf16[28,256,256]{2,1,0:T(8,128)(2,1)} async-done(((bf16[28,32,256]{2,1,0:T(8,128)(2,1)}), bf16[28,256,256]{2,1,0:T(8,128)(2,1)}) %all-gather.2.cloned.1.call-update) | async-done | bytes 3670032 | tf_op jit(solution)/shard_map/all_gather | solution.py:66
  70.1 5.2 scatter_fusion
  75.3 4.8 scatter_fusion.1
  80.1 4.8 scatter_fusion.2
  84.9 4.8 scatter_fusion.3
  89.7 4.8 scatter_fusion.4
  94.6 4.8 scatter_fusion.5
  99.3 4.8 scatter_fusion.6
  104.2 4.8 scatter_fusion.7
  109.0 4.8 scatter_fusion.8
  113.8 5.3 scatter_fusion.9
  119.0 4.8 scatter_fusion.10
  123.9 4.8 scatter_fusion.11
  128.6 4.8 scatter_fusion.12
  133.5 4.8 scatter_fusion.13
  138.3 4.8 scatter_fusion.14
  143.0 4.8 scatter_fusion.15
  147.9 4.8 scatter_fusion.16
  152.7 4.8 scatter_fusion.17
  157.5 4.8 scatter_fusion.18
  162.3 4.8 scatter_fusion.19
  167.1 4.9 scatter_fusion.20
  172.1 4.8 scatter_fusion.21
  176.9 4.8 scatter_fusion.22
  181.7 4.8 scatter_fusion.23
  186.5 4.8 scatter_fusion.24
  191.3 4.8 scatter_fusion.25
  196.1 4.8 scatter_fusion.26
  223.5 4.6 scatter_fusion.27
  228.8 41.0 %reduce-scatter.2.cloned.1.call-done = bf16[28,32,256]{2,1,0:T(8,128)(2,1)} async-done(((bf16[28,256,256]{2,1,0:T(8,128)(2,1)}), bf16[28,32,256]{2,1,0:T(8,128)(2,1)}) %reduce-scatter.2.cloned.1.call-update) | async-done | bytes 458768 | tf_op jit(solution)/shard_map/reduce_scatter | solution.py:79
  269.8 450.2 %all-reduce.2 = f32[28,32,256]{2,1,0:T(8,128)} all-reduce(bf16[28,32,256]{2,1,0:T(8,128)(2,1)} %reduce-scatter.2.cloned.1.call-done), channel_id=1, replica_groups=mesh['dp'=64,'shard'=8] {'dp'}, use_global_device_ids=true, to_apply=%region_29.30 | all-reduce | flops 229376 | bytes 1376256 | tf_op jit(solution)/shard_map/psum | solution.py:82
  (204 shorter events, 34.0 us)
Async XLA Ops:
  7.2 55.4 %all-gather.2.cloned.1.call-start = ((), (), s32[]{:S(2)}) async-start(), calls=%async_computation.1 | async-start | bytes 4128768 | tf_op jit(solution)/shard_map/all_gather | solution.py:66
  7.9 261.9 %reduce-scatter.2.cloned.1.call-start = ((), (), s32[]{:S(2)}) async-start(), calls=%async_computation.2 | async-start | bytes 4128768 | tf_op jit(solution)/shard_map/reduce_scatter | solution.py:79
  64.3 1.1 copy-start
  186.5 14.4 %copy-start.1 = (bf16[1,8,8,8,256]{4,3,2,1,0:T(8,128)(2,1)S(1)}, bf16[1,8,8,8,256]{4,3,2,1,0:T(8,128)(2,1)}, u32[]{:S(2)}) copy-start(bf16[1,8,8,8,256]{4,3,2,1,0:T(8,128)(2,1)} %param.3) | copy-start | bytes 786436
Sparse Core Ops, SparseCore 0:
  10.1 52.4 all-gather.1
  217.9 51.8 reduce-scatter.1
where the time goes:
time: 737 us; the launch traced here: 727 us
  blocking collectives  450 us (61%)
  other arithmetic  137 us (19%)
  waiting for transfers between devices  86.8 us (12%)
  local copies, waits for them, and re-layouts  25.5 us (3%)
  between operations  15.7 us (2%)
  matrix products  12.2 us (2%)
    psum x1, blocking collectives, shards(): weight_grad = lax.psum(owned, 'dp')  450 us
    scatter-add x27, other arithmetic, spread_back(): grid = grid.at[first:first + edge:2, second:second + edge:2, third:third...  131 us
    all_gather x1, waiting for transfers between devices, shards(): lax.all_gather(weights, 'shard', axis=1, tiled=True)  45.1 us
    reduce_scatter x1, waiting for transfers between devices, shards(): lax.psum_scatter(term.astype(jnp.bfloat16), 'shard', scatter_dimension=1,...  41 us
  transfers between devices with their start and end apart: 2, of which 2 were waited for; matrix products, arithmetic and copies ran while one was open for 3% of the time, Pallas kernels for 0%

commit v1 on v0

--- a/solution.py
+++ b/solution.py
@@ -63,7 +63,9 @@
     result = jnp.einsum(
         "qtc,tco->qo",
         cols,
-        lax.all_gather(weights, "shard", axis=1, tiled=True),
+        jnp.concatenate(
+            lax.all_to_all(jnp.stack([weights] * lax.axis_size("shard")), "shard", 0, 0), axis=1
+        ),
         preferred_element_type=jnp.float32,
     )
     grad_in = spread_back(

time: 737 us -> 811 us (1.10)
  waiting for transfers between devices: 86.8 us -> 148 us
  starting transfers between devices: 0.08 us -> 10.3 us
    all_gather x1, waiting for transfers between devices: 45.1 us -> 104 us  [shards(): lax.all_gather(weights, 'shard', axis=1, tiled=True)]
    all_to_all x0 -> x1, starting transfers between devices: none -> 10.3 us  [shards(): lax.all_to_all(jnp.stack([weights] * lax.axis_size('shard')), 'shard', 0, 0)]
  transfers between devices with their start and end apart: 2 -> 3, of which waited for: 2 -> 2; matrix products, arithmetic and copies ran while one was open for 3% -> 22% of each run, Pallas kernels for 0% -> 0%
where the time goes in v1:
time: 811 us; the launch traced here: 801 us
  blocking collectives  450 us (55%)
  waiting for transfers between devices  148 us (18%)
  other arithmetic  138 us (17%)
  local copies, waits for them, and re-layouts  28.3 us (3%)
  between operations  15.7 us (2%)
  starting transfers between devices  10.3 us (1%)
  matrix products  10.2 us (1%)
    psum x1, blocking collectives, shards(): weight_grad = lax.psum(owned, 'dp')  450 us
    scatter-add x27, other arithmetic, spread_back(): grid = grid.at[first:first + edge:2, second:second + edge:2, third:third...  132 us
    all_gather x1, waiting for transfers between devices, shards(): lax.all_gather(weights, 'shard', axis=1, tiled=True)  104 us
    reduce_scatter x1, waiting for transfers between devices, shards(): lax.psum_scatter(term.astype(jnp.bfloat16), 'shard', scatter_dimension=1,...  42.8 us
  transfers between devices with their start and end apart: 3, of which 2 were waited for; matrix products, arithmetic and copies ran while one was open for 22% of the time, Pallas kernels for 0%

profile of v1, /device:TPU:8, one launch (start us, length us, event | category | flops | bytes accessed | tf_op | source)
XLA Modules:
  0.0 800.7 jit_solution(5872317585293864474)
XLA Ops:
  11.3 10.3 %all-to-all-start = ((bf16[8,28,32,256]{3,2,1,0:T(8,128)(2,1)}), bf16[8,28,32,256]{3,2,1,0:T(8,128)(2,1)}, u32[]{:S(2)}, u32[]{:S(2)}) async-start(bf16[8,28,32,256]{3,2,1,0:T(8,128)(2,1)} %stack.185), calls=%async_computation | async-start | bytes 7340032 | tf_op jit(solution)/shard_map/all_to_all | solution.py:67
  25.6 104.4 %all-gather.2.cloned.1.call-done = bf16[28,256,256]{2,1,0:T(8,128)(2,1)} async-done(((bf16[28,32,256]{2,1,0:T(8,128)(2,1)}), bf16[28,256,256]{2,1,0:T(8,128)(2,1)}) %all-gather.2.cloned.1.call-update) | async-done | bytes 3670032 | tf_op jit(solution)/shard_map/all_gather | solution.py:72
  139.8 5.2 scatter_fusion
  145.1 5.2 scatter_fusion.1
  150.3 5.2 scatter_fusion.2
  155.5 5.2 scatter_fusion.3
  160.8 5.2 scatter_fusion.4
  166.0 4.8 scatter_fusion.5
  170.8 4.8 scatter_fusion.6
  175.6 4.8 scatter_fusion.7
  180.4 5.2 scatter_fusion.8
  185.7 4.8 scatter_fusion.9
  190.5 4.8 scatter_fusion.10
  195.3 4.8 scatter_fusion.11
  200.1 4.8 scatter_fusion.12
  204.9 4.8 scatter_fusion.13
  209.7 4.8 scatter_fusion.14
  214.5 4.8 scatter_fusion.15
  219.3 4.8 scatter_fusion.16
  224.1 4.8 scatter_fusion.17
  228.9 4.8 scatter_fusion.18
  233.7 5.0 scatter_fusion.19
  238.7 4.8 scatter_fusion.20
  243.5 4.8 scatter_fusion.21
  248.3 4.8 scatter_fusion.22
  253.1 4.8 scatter_fusion.23
  257.9 4.8 scatter_fusion.24
  262.7 4.8 scatter_fusion.25
  267.5 4.8 scatter_fusion.26
  295.4 4.6 scatter_fusion.27
  300.8 42.8 %reduce-scatter.2.cloned.1.call-done = bf16[28,32,256]{2,1,0:T(8,128)(2,1)} async-done(((bf16[28,256,256]{2,1,0:T(8,128)(2,1)}), bf16[28,32,256]{2,1,0:T(8,128)(2,1)}) %reduce-scatter.2.cloned.1.call-update) | async-done | bytes 458768 | tf_op jit(solution)/shard_map/reduce_scatter | solution.py:81
  343.6 450.1 %all-reduce.2 = f32[28,32,256]{2,1,0:T(8,128)} all-reduce(bf16[28,32,256]{2,1,0:T(8,128)(2,1)} %reduce-scatter.2.cloned.1.call-done), channel_id=1, replica_groups=mesh['dp'=64,'shard'=8] {'dp'}, use_global_device_ids=true, to_apply=%region_29.30 | all-reduce | flops 229376 | bytes 1376256 | tf_op jit(solution)/shard_map/psum | solution.py:84
  (210 shorter events, 40.6 us)
Async XLA Ops:
  7.2 122.8 %all-gather.2.cloned.1.call-start = ((), (), s32[]{:S(2)}) async-start(), calls=%async_computation.2 | async-start | bytes 4128768 | tf_op jit(solution)/shard_map/all_gather | solution.py:72
  11.3 10.3 %copy-start.1 = (bf16[1,8,8,8,256]{4,3,2,1,0:T(8,128)(2,1)S(1)}, bf16[1,8,8,8,256]{4,3,2,1,0:T(8,128)(2,1)}, u32[]{:S(2)}) copy-start(bf16[1,8,8,8,256]{4,3,2,1,0:T(8,128)(2,1)} %param.3) | copy-start | bytes 786436
  11.3 10.8 %copy-start = (bf16[1,4,4,4,256]{4,3,2,1,0:T(4,128)(2,1)S(1)}, bf16[1,4,4,4,256]{4,3,2,1,0:T(4,128)(2,1)}, u32[]{:S(2)}) copy-start(bf16[1,4,4,4,256]{4,3,2,1,0:T(4,128)(2,1)} %param.4) | copy-start | bytes 98308
  11.3 279.9 %all-to-all-start = ((bf16[8,28,32,256]{3,2,1,0:T(8,128)(2,1)}), bf16[8,28,32,256]{3,2,1,0:T(8,128)(2,1)}, u32[]{:S(2)}, u32[]{:S(2)}) async-start(bf16[8,28,32,256]{3,2,1,0:T(8,128)(2,1)} %stack.185), calls=%async_computation | async-start | bytes 7340032 | tf_op jit(solution)/shard_map/all_to_all | solution.py:67
  21.6 322.0 %reduce-scatter.2.cloned.1.call-start = ((), (), s32[]{:S(2)}) async-start(), calls=%async_computation.3 | async-start | bytes 4128768 | tf_op jit(solution)/shard_map/reduce_scatter | solution.py:81
  285.1 1.1 copy-start.2
Sparse Core Ops, SparseCore 0:
  10.1 119.8 all-gather.1
  289.4 54.1 reduce-scatter.1
